TPU v7x, 32 devices: a whole 2x2x4 slice. The times are simulated.
32 devices in a mesh: band: 4 (over z), roster: 8 (over y, x, core).
Axes of the slice: x: 2, y: 2, z: 4, core: 2. Of those that a mesh axis runs over, the one named last changes fastest.
Arguments:
- tiles: bfloat16 [4, 8, 6, 256, 256], P('band', 'roster'), as said below
- tile_slots: int32 [4, 8, 6], P('band', 'roster'), may hold values from 0 to 5, each once within a row
- tile_count: int32 [4, 8], P('band', 'roster'), may hold values from 1 to 6, as said below
- costs: float32 [6144, 128], P('roster'), may hold values from 1000 to 10000
- primal_start: float32 [6144, 128], P('roster'), may hold values from 0 to 1
- dual_start: float32 [2048, 128], P('band'), may hold values from 0.5 to 4
Outputs:
- primal: float32 [6144, 128], P('roster')
- dual: float32 [2048, 128], P('band')
Inputs may be any that keep to these rules, and one draw needn't show every extreme that they name: `tile_slots`: each device's slots list every tile position once; slot s is in use where s < tile_count. `tile_count`: some device uses all 6 slots. `tiles`: entries are zero or positive.
All inputs are finite; a program needn't handle non-finite values.
Results may differ from a plain program's by a relative error of at most 0.0003.
Values sent between devices are 32-bit elements; how exact they have to be, the bound alone decides.
A program may use at most 64 MiB of HBM per device.

v0:
```python
import functools

import jax
import jax.numpy as jnp
from jax import lax
from jax.experimental import pallas as pl
from jax.experimental.pallas import tpu as pltpu
from jax.sharding import PartitionSpec as P

ROUNDS = 3
ITERS = 4
eps = 1e-06
GROUPS = 2
CHUNK = 16
HOP = 1.7
LINK = 0.066
SUM = 4.4
START = 0.7
ROUND = 2.0
FROB = 6.0
SHIFT = 4.3
DOWN = 2.0**-24
UP = 2.0**24
MESH = pl.DeviceIdType.MESH
f32 = jnp.float32
bf16 = jnp.bfloat16


def kernel(
    cfg, slots_ref, count_ref, tiles_ref, cost_ref, x0_ref, y0_ref, primal_ref, dual_ref,
    a_ref, at_ref, cost_t, x_t, u_t, y_t, own, snd, rec, hown, hrec,
    rpeak_s, rpeak_r, cpeak_s, cpeak_r, fr_s, fr_r, fb_s, fb_r,
    rp_ss, rp_rs, cp_ss, cp_rs, fr_ss, fr_rs, fb_ss, fb_rs,
    g_ss, g_rs, rs_ss, rs_rs, ag_ss, ag_rs,
):
    nb, nr, groups, cs = cfg
    z = lax.axis_index("band")
    r = lax.axis_index("roster")
    slots = tiles_ref.shape[2]
    tile = tiles_ref.shape[3]
    rows, scen = y0_ref.shape
    cols = cost_ref.shape[0]
    col_tiles = cols // tile
    per = scen // groups
    kper = per // cs
    bs = max(8, per // nr)
    width = per * rows // (nr * bs)
    parts = rows // width

    def roster_peer(d):
        return (z, (r + d) % nr)

    def band_peer(d):
        return ((z + d) % nb, r)

    barrier = pltpu.get_barrier_semaphore()
    for d in range(1, nr):
        pl.semaphore_signal(barrier, inc=1, device_id=roster_peer(d), device_id_type=MESH)
    for d in range(1, nb):
        pl.semaphore_signal(barrier, inc=1, device_id=band_peer(d), device_id_type=MESH)

    for p in range(slots):
        at = jnp.int32(0)
        for s in range(slots):
            at = jnp.where(slots_ref[0, 0, s] == p, jnp.int32(s), at)
        factor = jnp.where(at < count_ref[0, 0], jnp.float32(DOWN), jnp.float32(0.0))
        block = tiles_ref[0, 0, at].astype(f32) * factor
        i, j = (p // col_tiles) * tile, (p % col_tiles) * tile
        a_ref[i : i + tile, j : j + tile] = block.astype(bf16)
        at_ref[j : j + tile, i : i + tile] = block.T.astype(bf16)

    def fold(ref, at, factor, op):
        part = ref[at : at + 128, :].astype(f32) * factor
        if op is jnp.add:
            part = part * part
        total = part[:, :128]
        for j in range(128, part.shape[1], 128):
            total = op(total, part[:, j : j + 128])
        return total.T

    def peaks(turn, row, col_up):
        for i in range(0, rows, 128):
            peak = jnp.max(fold(a_ref, i, col_up, jnp.maximum), axis=0, keepdims=True)
            rpeak_s[turn, :, i : i + 128] = peak * row[:, i : i + 128]
        for j in range(0, cols, 128):
            peak = jnp.max(fold(at_ref, j, row, jnp.maximum), axis=0, keepdims=True)
            cpeak_s[turn, :, j : j + 128] = peak * col_up[:, j : j + 128]

    def rpeak_copy(turn, d):
        return pltpu.make_async_remote_copy(
            rpeak_s.at[turn], rpeak_r.at[turn, d], rp_ss.at[turn, d], rp_rs.at[turn, d],
            device_id=roster_peer(d), device_id_type=MESH)

    def cpeak_copy(turn, d):
        return pltpu.make_async_remote_copy(
            cpeak_s.at[turn], cpeak_r.at[turn, d], cp_ss.at[turn, d], cp_rs.at[turn, d],
            device_id=band_peer(d), device_id_type=MESH)

    def peaks_send(turn):
        for d in range(1, nb):
            cpeak_copy(turn, d).start()
        for d in range(1, nr):
            rpeak_copy(turn, d).start()

    def peaks_wait(turn):
        row = rpeak_s[turn]
        col = cpeak_s[turn]
        for d in range(1, nr):
            rpeak_copy(turn, d).wait_recv()
            row = jnp.maximum(row, rpeak_r[turn, d])
        for d in range(1, nb):
            cpeak_copy(turn, d).wait_recv()
            col = jnp.maximum(col, cpeak_r[turn, d])
        return row, col

    def fr_copy(d):
        return pltpu.make_async_remote_copy(
            fr_s, fr_r.at[d], fr_ss.at[d], fr_rs.at[d],
            device_id=roster_peer(d), device_id_type=MESH)

    def fb_copy(d):
        return pltpu.make_async_remote_copy(
            fb_s, fb_r.at[d], fb_ss.at[d], fb_rs.at[d],
            device_id=band_peer(d), device_id_type=MESH)

    is_end = (z == 0) | (z == nb - 1)
    inner = (z > 0) & (z < nb - 1)
    lead = (z * 2) // nb
    back = 1 - lead

    def split_dot(value, matrix):
        high = value.astype(bf16)
        low = (value - high.astype(f32)).astype(bf16)
        both = jnp.dot(jnp.concatenate([high, low], 0), matrix, preferred_element_type=f32)
        return both[: value.shape[0]] + both[value.shape[0] :]

    def g_copy(par, way, k):
        at = pl.ds(k * cs, cs)
        return pltpu.make_async_remote_copy(
            snd.at[way, at], rec.at[par, way, at], g_ss.at[way, k], g_rs.at[par, way, k],
            device_id=((z + nb + 1 - 2 * way) % nb, r), device_id_type=MESH)

    def g_sent(grp, par):
        for k in range(grp * kper, (grp + 1) * kper):
            g_copy(par, lead, k).wait_send()

        @pl.when(inner)
        def _():
            for k in range(grp * kper, (grp + 1) * kper):
                g_copy(par, back, k).wait_send()

    def g_start(grp, t):
        if t > 0:
            g_sent(grp, (t - 1) % 2)
        at = pl.ds(grp * per, per)
        value = split_dot(y_t[at, :], a_ref[...])
        own[at, :] = value

        @pl.when(is_end)
        def _():
            snd[lead, at, :] = value
            for k in range(grp * kper, (grp + 1) * kper):
                g_copy(t % 2, lead, k).start()

    def first(t, k):
        @pl.when(inner)
        def _():
            at = pl.ds(k * cs, cs)
            g_copy(t % 2, lead, k).wait_recv()
            snd[lead, at, :] = rec[t % 2, lead, at, :] + own[at, :]
            g_copy(t % 2, lead, k).start()

    def second(t, k):
        g_copy(t % 2, back, k).wait_recv()

        @pl.when(inner)
        def _():
            at = pl.ds(k * cs, cs)
            snd[back, at, :] = rec[t % 2, back, at, :] + own[at, :]
            g_copy(t % 2, back, k).start()

    def block_at(grp, q):
        if parts == 1:
            return (pl.ds(pl.multiple_of(grp * per + q * bs, 8), bs), slice(None))
        return (
            pl.ds(pl.multiple_of(grp * per + (q // parts) * bs, 8), bs),
            pl.ds(pl.multiple_of((q % parts) * width, 128), width),
        )

    def rs_copy(grp, d):
        return pltpu.make_async_remote_copy(
            hown.at[block_at(grp, (r + d) % nr)], hrec.at[grp, d],
            rs_ss.at[grp, d], rs_rs.at[grp, d],
            device_id=roster_peer(d), device_id_type=MESH)

    def ag_copy(grp, d):
        here = block_at(grp, r)
        return pltpu.make_async_remote_copy(
            y_t.at[here], y_t.at[here], ag_ss.at[grp, d], ag_rs.at[grp, d],
            device_id=roster_peer(d), device_id_type=MESH)

    def ag_arrived(grp, d):
        here = block_at(grp, (r + nr - d) % nr)
        return pltpu.make_async_remote_copy(
            y_t.at[here], y_t.at[here], ag_ss.at[grp, d], ag_rs.at[grp, d],
            device_id=roster_peer(d), device_id_type=MESH)

    order = sorted(range(1, nr), key=lambda d: -bin(d).count("1"))

    one_row = jnp.ones((1, rows), f32)
    one_col = jnp.ones((1, cols), f32)
    row, col_up = one_row, one_col * UP
    peaks(0, row, col_up)
    pl.semaphore_wait(barrier, nr - 1 + nb - 1)
    peaks_send(0)
    for i in range(0, rows, 128):
        y_t[:, i : i + 128] = y0_ref[i : i + 128, :].T
    for grp in range(groups):
        g_start(grp, 0)

    state = dict(row=row, col_up=col_up)

    def equilibrate(turn):
        if turn == 0:
            for j in range(0, cols, 128):
                cost_t[:, j : j + 128] = cost_ref[j : j + 128, :].T
                x_t[:, j : j + 128] = x0_ref[j : j + 128, :].T
        row_peak, col_peak = peaks_wait(turn)
        state["row"] = state["row"] / jnp.sqrt(row_peak + eps)
        state["col_up"] = state["col_up"] / jnp.sqrt(col_peak + eps)
        if turn + 1 < ROUNDS:
            peaks(turn + 1, state["row"], state["col_up"])
            peaks_send(turn + 1)
        else:
            squares_start()

    def squares_start():
        row, col_up = state["row"], state["col_up"]
        col = state["col"] = col_up * DOWN
        state["row_up"] = row * UP
        squares = jnp.zeros((1, 128), f32)
        for j in range(0, cols, 128):
            part = jnp.sum(fold(at_ref, j, row, jnp.add), axis=0, keepdims=True)
            scale = col_up[:, j : j + 128]
            squares = squares + part * scale * scale
        fr_s[...] = squares
        for d in range(1, nr):
            fr_copy(d).start()
        for j in range(0, cols, 128):
            cost_t[:, j : j + 128] = cost_t[:, j : j + 128] * col[:, j : j + 128]
        state["squares"] = squares

    def squares_mid():
        squares = state["squares"]
        for d in range(1, nr):
            fr_copy(d).wait_recv()
            squares = squares + fr_r[d]
        fb_s[...] = squares
        for d in range(1, nb):
            fb_copy(d).start()
        state["squares"] = squares

    def squares_end():
        squares = state["squares"]
        for d in range(1, nb):
            fb_copy(d).wait_recv()
            squares = squares + fb_r[d]
        eta = 0.9 / jnp.sqrt(jnp.sum(squares, axis=1, keepdims=True) + eps)
        state["eta_col"] = eta * state["col"]
        state["eta_row"] = eta * state["row"]

    def update(t, k):
        at = pl.ds(k * cs, cs)
        total = snd[lead, at, :] + rec[t % 2, back, at, :]
        before = x_t[at, :]
        eta_col, col_up = state["eta_col"], state["col_up"]
        after = jnp.clip(before - eta_col * (cost_t[at, :] - col_up * total), 0.0, 1.0)
        x_t[at, :] = after
        u_t[at, :] = 2.0 * after - before

    def h_start(grp, t):
        if t > 0:
            for d in order:
                rs_copy(grp, d).wait_send()
        at = pl.ds(grp * per, per)
        hown[at, :] = split_dot(u_t[at, :], at_ref[...])
        for d in order:
            rs_copy(grp, d).start()

    def h_mid(grp, t):
        here = block_at(grp, r)
        row, row_up, eta_row = state["row"], state["row_up"], state["eta_row"]
        total = hown[here]
        for d in range(1, nr):
            rs_copy(grp, d).wait_recv()
            total = total + hrec[grp, d]
        if t > 0:
            for d in order:
                ag_copy(grp, d).wait_send()
        if parts == 1:
            y_t[here] = y_t[here] + eta_row * (row - row_up * total)
        else:
            lane = (r % parts) * width
            own_row = jnp.zeros((1, width), f32)
            own_eta = jnp.zeros((1, width), f32)
            for q in range(parts):
                mine = lane == q * width
                own_row = jnp.where(mine, row[:, q * width : (q + 1) * width], own_row)
                own_eta = jnp.where(mine, eta_row[:, q * width : (q + 1) * width], own_eta)
            y_t[here] = y_t[here] + own_eta * (own_row - (own_row * UP) * total)
        for d in order:
            ag_copy(grp, d).start()

    def h_fin(grp):
        for d in range(1, nr):
            ag_arrived(grp, d).wait_recv()

    plan = []

    def put(when, step, *args):
        plan.append((when, len(plan), functools.partial(step, *args)))

    unit = LINK * cs
    for turn in range(ROUNDS):
        put(ROUND * (turn + 1), equilibrate, turn)
    put(ROUND * ROUNDS + FROB / 2, squares_mid)
    ready = ROUND * ROUNDS + FROB
    put(ready, squares_end)
    for grp in range(groups):
        ks = range(grp * kper, (grp + 1) * kper)
        for k in ks:
            put(START + unit * (k + 1) + HOP, first, 0, k)
            put(START + unit * (k + 2) + 2 * HOP, second, 0, k)
        begin = max(ready, START + unit * (kper + 2) + 3 * HOP) + grp * SHIFT
        for t in range(ITERS):
            if t > 0:
                for i, k in enumerate(ks):
                    put(begin + unit * (i + 1) + HOP, first, t, k)
                    put(begin + unit * (i + 2) + 2 * HOP, second, t, k)
                    put(begin + unit * (i + 2) + 2 * HOP, update, t, k)
                begin = begin + unit * (kper + 2) + 3 * HOP
            else:
                for k in ks:
                    put(begin, update, t, k)
            put(begin, h_start, grp, t)
            put(begin + SUM, h_mid, grp, t)
            put(begin + 2 * SUM, h_fin, grp)
            if t + 1 < ITERS:
                put(begin + 2 * SUM, g_start, grp, t + 1)
            begin = begin + 2 * SUM + START
    for when, index, step in sorted(plan, key=lambda entry: entry[:2]):
        step()
    row, col = state["row"], state["col"]

    for j in range(0, cols, 128):
        primal_ref[j : j + 128, :] = (x_t[:, j : j + 128] / col[:, j : j + 128]).T
    for i in range(0, rows, 128):
        dual_ref[i : i + 128, :] = (y_t[:, i : i + 128] / row[:, i : i + 128]).T

    for grp in range(groups):
        g_sent(grp, (ITERS - 1) % 2)
        for d in order:
            rs_copy(grp, d).wait_send()
            ag_copy(grp, d).wait_send()
    for d in range(1, nr):
        fr_copy(d).wait_send()
        for turn in range(ROUNDS):
            rpeak_copy(turn, d).wait_send()
    for d in range(1, nb):
        fb_copy(d).wait_send()
        for turn in range(ROUNDS):
            cpeak_copy(turn, d).wait_send()


def shards(nb, nr, tiles, tile_slots, tile_count, costs, primal_start, dual_start):
    rows, scen = dual_start.shape
    cols = costs.shape[0]
    groups = GROUPS if (scen // GROUPS) * rows // nr >= 1024 else 1
    cs = CHUNK
    chunks = scen // cs
    per = scen // groups
    bs = max(8, per // nr)
    width = per * rows // (nr * bs)
    vmem = pl.BlockSpec(memory_space=pltpu.VMEM)
    smem = pl.BlockSpec(memory_space=pltpu.SMEM)
    dma = pltpu.SemaphoreType.DMA
    return pl.pallas_call(
        functools.partial(kernel, (nb, nr, groups, cs)),
        name="primal_dual",
        out_shape=(
            jax.ShapeDtypeStruct((cols, scen), f32),
            jax.ShapeDtypeStruct((rows, scen), f32),
        ),
        in_specs=[smem, smem, vmem, vmem, vmem, vmem],
        out_specs=(vmem, vmem),
        scratch_shapes=[
            pltpu.VMEM((rows, cols), bf16),
            pltpu.VMEM((cols, rows), bf16),
            pltpu.VMEM((scen, cols), f32),
            pltpu.VMEM((scen, cols), f32),
            pltpu.VMEM((scen, cols), f32),
            pltpu.VMEM((scen, rows), f32),
            pltpu.VMEM((scen, cols), f32),
            pltpu.VMEM((2, scen, cols), f32),
            pltpu.VMEM((2, 2, scen, cols), f32),
            pltpu.VMEM((scen, rows), f32),
            pltpu.VMEM((groups, nr, bs, width), f32),
            pltpu.VMEM((ROUNDS, 1, rows), f32),
            pltpu.VMEM((ROUNDS, nr, 1, rows), f32),
            pltpu.VMEM((ROUNDS, 1, cols), f32),
            pltpu.VMEM((ROUNDS, nb, 1, cols), f32),
            pltpu.VMEM((1, 128), f32),
            pltpu.VMEM((nr, 1, 128), f32),
            pltpu.VMEM((1, 128), f32),
            pltpu.VMEM((nb, 1, 128), f32),
            dma((ROUNDS, nr)),
            dma((ROUNDS, nr)),
            dma((ROUNDS, nb)),
            dma((ROUNDS, nb)),
            dma((nr,)),
            dma((nr,)),
            dma((nb,)),
            dma((nb,)),
            dma((2, chunks)),
            dma((2, 2, chunks)),
            dma((groups, nr)),
            dma((groups, nr)),
            dma((groups, nr)),
            dma((groups, nr)),
        ],
        compiler_params=pltpu.CompilerParams(collective_id=0, has_side_effects=True),
    )(tile_slots, tile_count, tiles, costs, primal_start, dual_start)


def solution(mesh):
    placed = (
        P("band", "roster", None, None, None),
        P("band", "roster", None),
        P("band", "roster"),
        P("roster", None),
        P("roster", None),
        P("band", None),
    )
    return jax.shard_map(
        functools.partial(shards, mesh.shape["band"], mesh.shape["roster"]),
        mesh=mesh,
        in_specs=placed,
        out_specs=(P("roster", None), P("band", None)),
        check_vma=False,
    )
```

profile of v0, /device:TPU:0, one launch (start us, length us, event | category | flops | bytes accessed | tf_op | source)
XLA Modules:
  0.0 119.2 jit_solution(11754335222420352801)
XLA Ops:
  1.3 115.4 %primal_dual.1 = (f32[768,128]{1,0:T(8,128)}, f32[512,128]{1,0:T(8,128)}) custom-call(s32[1,1,6]{2,1,0:T(1,128)} %slots_ref.1, s32[1,1]{1,0:T(1,128)S(6)} %copy.10.count_ref, bf16[1,1,6,256,256]{4,3,2,1,0:T(8,128)(2,1)} %tiles_ref.1, f32[768,128]{1,0:T(8,128)} %cost_ref.1, f32[768,128]{1,0:T(8,128)} %x0_ref.1, f32[512,128]{1,0:T(8,128)} %y0_ref.1), custom_call_target="tpu_custom_call" | custom-call | tf_op jit(solution)/shard_map/primal_dual/pallas_call | solution.py:387
  116.7 0.0 copy-start
  116.7 1.8 %copy.11 = f32[768,128]{1,0:T(8,128)} copy(f32[768,128]{1,0:T(8,128)} %get-tuple-element.4) | data formatting | bytes 786432
  118.5 0.0 copy-done
  118.5 0.7 copy.12
Async XLA Ops:
  116.7 1.8 %copy-start = (f32[512,128]{1,0:T(8,128)S(1)}, f32[512,128]{1,0:T(8,128)}, u32[]{:S(2)}) copy-start(f32[512,128]{1,0:T(8,128)} %get-tuple-element.5) | copy-start | bytes 786436
where the time goes:
time: 119 us
  Pallas kernels  115 us (97%)
  local copies, waits for them, and re-layouts  2.52 us (2%)
  between operations  1.29 us (1%)
    pallas_call x1, Pallas kernels, shards(): pl.pallas_call(functools.partial(kernel, (nb, nr, groups, cs)), name='pri...  115 us
    unnamed x4, local copies, waits for them, and re-layouts  2.52 us

commit v1 on v0

v1 whole, which is shorter than its diff:
```python
import functools

import jax
import jax.numpy as jnp
from jax import lax
from jax.experimental import pallas as pl
from jax.experimental.pallas import tpu as pltpu
from jax.sharding import PartitionSpec as P

ROUNDS = 3
ITERS = 4
eps = 1e-06
GROUPS = 4
SHIFT = 2.0
SCATTER = 4.6
GATHER = 4.6
CAST = 4.0
DOWN = 2.0**-24
UP = 2.0**24
MESH = pl.DeviceIdType.MESH
f32 = jnp.float32
bf16 = jnp.bfloat16


def kernel(
    cfg, slots_ref, count_ref, tiles_ref, cost_ref, x0_ref, y0_ref, primal_ref, dual_ref,
    a_ref, at_ref, tile_s, tile_r, stage, cost_t, x_t, y_t, part, blocks, casts, fin, yfin,
    rpeak_s, rpeak_r, cpeak_s, cpeak_r, fr_s, fr_r, fb_s, fb_r, col_s, col_r, cols_v,
    rp_ss, rp_rs, cp_ss, cp_rs, fr_ss, fr_rs, fb_ss, fb_rs,
    rs_ss, rs_rs, ag_ss, ag_rs, h_ss, h_rs, pair_ss, pair_rs, xf_ss, xf_rs, yf_ss, yf_rs,
):
    nb, nr, groups = cfg
    z = lax.axis_index("band")
    r = lax.axis_index("roster")
    core = r % 2
    chip = r // 2
    chips = nr // 2
    slots = tiles_ref.shape[2]
    tile = tiles_ref.shape[3]
    rows, scen = y0_ref.shape
    cols = cost_ref.shape[0]
    col_tiles = cols // tile
    half = scen // 2
    per = half // groups
    both = 2 * cols
    width = both // nb

    def roster_peer(d):
        return (z, (r + d) % nr)

    def band_peer(d):
        return ((z + d) % nb, r)

    def chip_peer(d):
        return (z, 2 * ((chip + d) % chips) + core)

    partner = (z, r + 1 - 2 * core)

    barrier = pltpu.get_barrier_semaphore()
    for d in range(1, nr):
        pl.semaphore_signal(barrier, inc=1, device_id=roster_peer(d), device_id_type=MESH)
    for d in range(1, nb):
        pl.semaphore_signal(barrier, inc=1, device_id=band_peer(d), device_id_type=MESH)

    def build():
        for p in range(slots):
            at = jnp.int32(0)
            for s in range(slots):
                at = jnp.where(slots_ref[0, 0, s] == p, jnp.int32(s), at)
            factor = jnp.where(at < count_ref[0, 0], jnp.float32(DOWN), jnp.float32(0.0))
            block = tiles_ref[0, 0, at].astype(f32) * factor
            i, j = (p // col_tiles) * tile, (p % col_tiles) * tile
            tile_s[i : i + tile, j : j + tile] = block
            a_ref[i : i + tile, j : j + tile] = block.astype(bf16)
            at_ref[j : j + tile, i : i + tile] = block.T.astype(bf16)

    def fold(ref, at, span, factor, op):
        part = ref[at : at + 128, :span].astype(f32) * factor
        if op is jnp.add:
            part = part * part
        total = part[:, :128]
        for j in range(128, part.shape[1], 128):
            total = op(total, part[:, j : j + 128])
        return total.T

    def peaks(turn, row, col_up):
        for i in range(0, rows, 128):
            peak = jnp.max(fold(a_ref, i, cols, col_up, jnp.maximum), axis=0, keepdims=True)
            rpeak_s[turn, :, i : i + 128] = peak * row[:, i : i + 128]
        for j in range(0, cols, 128):
            peak = jnp.max(fold(at_ref, j, rows, row, jnp.maximum), axis=0, keepdims=True)
            cpeak_s[turn, :, j : j + 128] = peak * col_up[:, j : j + 128]

    def rpeak_copy(turn, d):
        return pltpu.make_async_remote_copy(
            rpeak_s.at[turn], rpeak_r.at[turn, d], rp_ss.at[turn, d], rp_rs.at[turn, d],
            device_id=roster_peer(d), device_id_type=MESH)

    def cpeak_copy(turn, d):
        return pltpu.make_async_remote_copy(
            cpeak_s.at[turn], cpeak_r.at[turn, d], cp_ss.at[turn, d], cp_rs.at[turn, d],
            device_id=band_peer(d), device_id_type=MESH)

    def peaks_send(turn):
        for d in range(1, nb):
            cpeak_copy(turn, d).start()
        for d in range(1, nr):
            rpeak_copy(turn, d).start()

    def peaks_wait(turn):
        row = rpeak_s[turn]
        col = cpeak_s[turn]
        for d in range(1, nr):
            rpeak_copy(turn, d).wait_recv()
            row = jnp.maximum(row, rpeak_r[turn, d])
        for d in range(1, nb):
            cpeak_copy(turn, d).wait_recv()
            col = jnp.maximum(col, cpeak_r[turn, d])
        return row, col

    def fr_copy(d):
        return pltpu.make_async_remote_copy(
            fr_s, fr_r.at[d], fr_ss.at[d], fr_rs.at[d],
            device_id=roster_peer(d), device_id_type=MESH)

    def fb_copy(d):
        return pltpu.make_async_remote_copy(
            fb_s, fb_r.at[d], fb_ss.at[d], fb_rs.at[d],
            device_id=band_peer(d), device_id_type=MESH)

    mine = pl.ds(pl.multiple_of(core * half, 8), half)
    theirs = pl.ds(pl.multiple_of((1 - core) * half, 8), half)

    def pair_copy(i, src, dst):
        return pltpu.make_async_remote_copy(
            src, dst, pair_ss.at[i], pair_rs.at[i], device_id=partner, device_id_type=MESH)

    def tile_copy():
        return pair_copy(0, tile_s, tile_r)

    def start_copy(i):
        dst = cost_t if i == 0 else x_t.at[0]
        return pair_copy(1 + i, stage.at[i, theirs], dst.at[:, cols:])

    def scale_copy():
        return pair_copy(3, col_s, col_r)

    def block_of(k):
        return pl.ds(pl.multiple_of(k * width, 128), width)

    def of(grp):
        return pl.ds(grp * per, per)

    def rs_copy(grp, d):
        return pltpu.make_async_remote_copy(
            part.at[of(grp), block_of((z + d) % nb)], blocks.at[d, of(grp)],
            rs_ss.at[grp, d], rs_rs.at[grp, d],
            device_id=band_peer(d), device_id_type=MESH)

    def ag_copy(grp, t, d):
        here = x_t.at[(t + 1) % 2, of(grp), block_of(z)]
        return pltpu.make_async_remote_copy(
            here, here, ag_ss.at[grp, d], ag_rs.at[grp, d],
            device_id=band_peer(d), device_id_type=MESH)

    def ag_arrived(grp, t, d):
        here = x_t.at[(t + 1) % 2, of(grp), block_of((z + nb - d) % nb)]
        return pltpu.make_async_remote_copy(
            here, here, ag_ss.at[grp, d], ag_rs.at[grp, d],
            device_id=band_peer(d), device_id_type=MESH)

    def h_copy(grp, t, d):
        here = casts.at[t % 2, chip, of(grp)]
        return pltpu.make_async_remote_copy(
            here, here, h_ss.at[grp, d], h_rs.at[t % 2, grp, d],
            device_id=chip_peer(d), device_id_type=MESH)

    def h_arrived(grp, t, d):
        here = casts.at[t % 2, (chip + chips - d) % chips, of(grp)]
        return pltpu.make_async_remote_copy(
            here, here, h_ss.at[grp, d], h_rs.at[t % 2, grp, d],
            device_id=chip_peer(d), device_id_type=MESH)

    def final_at(grp):
        return pl.ds(pl.multiple_of(core * half + grp * per, 8), per)

    def xf_copy(grp):
        return pltpu.make_async_remote_copy(
            x_t.at[ITERS % 2, of(grp), cols:], fin.at[final_at(grp)],
            xf_ss.at[grp], xf_rs.at[grp], device_id=partner, device_id_type=MESH)

    def yf_copy(grp):
        return pltpu.make_async_remote_copy(
            y_t.at[of(grp)], yfin.at[final_at(grp)],
            yf_ss.at[grp], yf_rs.at[grp], device_id=partner, device_id_type=MESH)

    def split_dot(value, matrix):
        high = value.astype(bf16)
        low = (value - high.astype(f32)).astype(bf16)
        both = jnp.dot(jnp.concatenate([high, low], 0), matrix, preferred_element_type=f32)
        return both[: value.shape[0]] + both[value.shape[0] :]

    far = range(nb - 1, 0, -1)
    state = {}

    def begin():
        state["row"] = jnp.ones((1, rows), f32)
        state["col_up"] = jnp.ones((1, cols), f32) * UP
        build()
        peaks(0, state["row"], state["col_up"])
        pl.semaphore_wait(barrier, nr - 1 + nb - 1)
        peaks_send(0)
        tile_copy().start()

    def starts():
        for i, ref in enumerate((cost_ref, x0_ref)):
            for j in range(0, cols, 128):
                stage[i, :, j : j + 128] = ref[j : j + 128, :].T
            start_copy(i).start()
        cost_t[:, :cols] = stage[0, mine]
        x_t[0, :, :cols] = stage[1, mine]
        for i in range(0, rows, 128):
            yfin[:, i : i + 128] = y0_ref[i : i + 128, :].T
        y_t[...] = yfin[mine]

    def tiles_in():
        tile_copy().wait_recv()
        for i in range(0, rows, tile):
            for j in range(0, cols, tile):
                block = tile_r[i : i + tile, j : j + tile]
                a_ref[i : i + tile, cols + j : cols + j + tile] = block.astype(bf16)
                at_ref[cols + j : cols + j + tile, i : i + tile] = block.T.astype(bf16)

    def starts_in():
        for i in range(2):
            start_copy(i).wait_recv()

    def equilibrate(turn):
        row_peak, col_peak = peaks_wait(turn)
        state["row"] = state["row"] / jnp.sqrt(row_peak + eps)
        state["col_up"] = state["col_up"] / jnp.sqrt(col_peak + eps)
        if turn + 1 < ROUNDS:
            peaks(turn + 1, state["row"], state["col_up"])
            peaks_send(turn + 1)
        else:
            squares_start()

    def squares_start():
        row, col_up = state["row"], state["col_up"]
        col_s[...] = col_up
        scale_copy().start()
        state["row_up"] = row * UP
        squares = jnp.zeros((1, 128), f32)
        for j in range(0, cols, 128):
            part = jnp.sum(fold(at_ref, j, rows, row, jnp.add), axis=0, keepdims=True)
            scale = col_up[:, j : j + 128]
            squares = squares + part * scale * scale
        fr_s[...] = squares
        for d in range(1, nr):
            fr_copy(d).start()
        state["squares"] = squares

    def squares_mid():
        squares = state["squares"]
        for d in range(1, nr):
            fr_copy(d).wait_recv()
            squares = squares + fr_r[d]
        fb_s[...] = squares
        for d in range(1, nb):
            fb_copy(d).start()
        state["squares"] = squares

    def scales_in():
        scale_copy().wait_recv()
        cols_v[:, :cols] = state["col_up"]
        cols_v[:, cols:] = col_r[...]
        state["up"] = cols_v[:, block_of(z)]
        col = state["up"] * DOWN
        cost_t[:, block_of(z)] = cost_t[:, block_of(z)] * col

    def squares_end():
        squares = state["squares"]
        for d in range(1, nb):
            fb_copy(d).wait_recv()
            squares = squares + fb_r[d]
        eta = 0.9 / jnp.sqrt(jnp.sum(squares, axis=1, keepdims=True) + eps)
        state["eta_col"] = eta * (state["up"] * DOWN)
        state["eta_row"] = eta * state["row"]

    def scatter(grp, t):
        if t > 0:
            for d in far:
                rs_copy(grp, d).wait_send()
        part[of(grp), :] = split_dot(y_t[of(grp), :], a_ref[...])
        for d in far:
            rs_copy(grp, d).start()

    def update(grp, t):
        total = part[of(grp), block_of(z)]
        for d in range(1, nb):
            rs_copy(grp, d).wait_recv()
            total = total + blocks[d, of(grp)]
        if t > 0:
            for d in far:
                ag_copy(grp, t - 1, d).wait_send()
        before = x_t[t % 2, of(grp), block_of(z)]
        cost = cost_t[of(grp), block_of(z)]
        move = state["eta_col"] * (cost - state["up"] * total)
        x_t[(t + 1) % 2, of(grp), block_of(z)] = jnp.clip(before - move, 0.0, 1.0)
        for d in far:
            ag_copy(grp, t, d).start()

    def cast(grp, t):
        for d in range(1, nb):
            ag_arrived(grp, t, d).wait_recv()
        after = x_t[(t + 1) % 2, of(grp), :]
        value = 2.0 * after - x_t[t % 2, of(grp), :]
        if t > 0:
            for d in range(1, chips):
                h_copy(grp, t - 1, d).wait_send()
        casts[t % 2, chip, of(grp)] = split_dot(value, at_ref[...])
        for d in range(1, chips):
            h_copy(grp, t, d).start()
        if t + 1 == ITERS:
            xf_copy(grp).start()

    def rise(grp, t):
        for d in range(1, chips):
            h_arrived(grp, t, d).wait_recv()
        total = casts[t % 2, 0, of(grp)]
        for k in range(1, chips):
            total = total + casts[t % 2, k, of(grp)]
        row, row_up, eta_row = state["row"], state["row_up"], state["eta_row"]
        y_t[of(grp), :] = y_t[of(grp), :] + eta_row * (row - row_up * total)
        if t + 1 < ITERS:
            scatter(grp, t + 1)
        else:
            yf_copy(grp).start()

    begin()
    starts()
    equilibrate(0)
    tiles_in()
    for grp in range(groups // 2):
        scatter(grp, 0)
    equilibrate(1)
    for grp in range(groups // 2, groups):
        scatter(grp, 0)
    starts_in()
    equilibrate(2)
    squares_mid()
    scales_in()
    squares_end()

    plan = []

    def put(when, step, *args):
        plan.append((when, len(plan), functools.partial(step, *args)))

    for grp in range(groups):
        when = grp * SHIFT
        for t in range(ITERS):
            put(when, update, grp, t)
            when += GATHER
            put(when, cast, grp, t)
            when += CAST
            put(when, rise, grp, t)
            when += SCATTER
    for when, index, step in sorted(plan, key=lambda entry: entry[:2]):
        step()

    col = state["col_up"] * DOWN
    row = state["row"]
    fin[mine, :] = x_t[ITERS % 2, :, :cols]
    for grp in range(groups):
        xf_copy(grp).wait_recv()
    for j in range(0, cols, 128):
        primal_ref[j : j + 128, :] = (fin[:, j : j + 128] / col[:, j : j + 128]).T
    yfin[mine, :] = y_t[...]
    for grp in range(groups):
        yf_copy(grp).wait_recv()
    for i in range(0, rows, 128):
        dual_ref[i : i + 128, :] = (yfin[:, i : i + 128] / row[:, i : i + 128]).T

    tile_copy().wait_send()
    scale_copy().wait_send()
    for i in range(2):
        start_copy(i).wait_send()
    for grp in range(groups):
        xf_copy(grp).wait_send()
        yf_copy(grp).wait_send()
        for d in far:
            rs_copy(grp, d).wait_send()
            ag_copy(grp, ITERS - 1, d).wait_send()
        for d in range(1, chips):
            h_copy(grp, ITERS - 1, d).wait_send()
    for d in range(1, nr):
        fr_copy(d).wait_send()
        for turn in range(ROUNDS):
            rpeak_copy(turn, d).wait_send()
    for d in range(1, nb):
        fb_copy(d).wait_send()
        for turn in range(ROUNDS):
            cpeak_copy(turn, d).wait_send()


def shards(nb, nr, tiles, tile_slots, tile_count, costs, primal_start, dual_start):
    rows, scen = dual_start.shape
    cols = costs.shape[0]
    groups = GROUPS
    half = scen // 2
    both = 2 * cols
    chips = nr // 2
    vmem = pl.BlockSpec(memory_space=pltpu.VMEM)
    smem = pl.BlockSpec(memory_space=pltpu.SMEM)
    dma = pltpu.SemaphoreType.DMA
    return pl.pallas_call(
        functools.partial(kernel, (nb, nr, groups)),
        name="primal_dual",
        out_shape=(
            jax.ShapeDtypeStruct((cols, scen), f32),
            jax.ShapeDtypeStruct((rows, scen), f32),
        ),
        in_specs=[smem, smem, vmem, vmem, vmem, vmem],
        out_specs=(vmem, vmem),
        scratch_shapes=[
            pltpu.VMEM((rows, both), bf16),
            pltpu.VMEM((both, rows), bf16),
            pltpu.VMEM((rows, cols), f32),
            pltpu.VMEM((rows, cols), f32),
            pltpu.VMEM((2, scen, cols), f32),
            pltpu.VMEM((half, both), f32),
            pltpu.VMEM((2, half, both), f32),
            pltpu.VMEM((half, rows), f32),
            pltpu.VMEM((half, both), f32),
            pltpu.VMEM((nb, half, both // nb), f32),
            pltpu.VMEM((2, chips, half, rows), f32),
            pltpu.VMEM((scen, cols), f32),
            pltpu.VMEM((scen, rows), f32),
            pltpu.VMEM((ROUNDS, 1, rows), f32),
            pltpu.VMEM((ROUNDS, nr, 1, rows), f32),
            pltpu.VMEM((ROUNDS, 1, cols), f32),
            pltpu.VMEM((ROUNDS, nb, 1, cols), f32),
            pltpu.VMEM((1, 128), f32),
            pltpu.VMEM((nr, 1, 128), f32),
            pltpu.VMEM((1, 128), f32),
            pltpu.VMEM((nb, 1, 128), f32),
            pltpu.VMEM((1, cols), f32),
            pltpu.VMEM((1, cols), f32),
            pltpu.VMEM((1, both), f32),
            dma((ROUNDS, nr)),
            dma((ROUNDS, nr)),
            dma((ROUNDS, nb)),
            dma((ROUNDS, nb)),
            dma((nr,)),
            dma((nr,)),
            dma((nb,)),
            dma((nb,)),
            dma((groups, nb)),
            dma((groups, nb)),
            dma((groups, nb)),
            dma((groups, nb)),
            dma((groups, chips)),
            dma((2, groups, chips)),
            dma((4,)),
            dma((4,)),
            dma((groups,)),
            dma((groups,)),
            dma((groups,)),
            dma((groups,)),
        ],
        compiler_params=pltpu.CompilerParams(collective_id=0, has_side_effects=True),
    )(tile_slots, tile_count, tiles, costs, primal_start, dual_start)


def solution(mesh):
    placed = (
        P("band", "roster", None, None, None),
        P("band", "roster", None),
        P("band", "roster"),
        P("roster", None),
        P("roster", None),
        P("band", None),
    )
    return jax.shard_map(
        functools.partial(shards, mesh.shape["band"], mesh.shape["roster"]),
        mesh=mesh,
        in_specs=placed,
        out_specs=(P("roster", None), P("band", None)),
        check_vma=False,
    )
```

time: 119 us -> 101 us (0.85)
  Pallas kernels: 115 us -> 97.3 us
    pallas_call x1, Pallas kernels: 115 us -> 97.3 us  [shards(): pl.pallas_call(functools.partial(kernel, (nb, nr, groups)), name='primal_...]
where the time goes in v1:
time: 101 us
  Pallas kernels  97.3 us (96%)
  local copies, waits for them, and re-layouts  2.52 us (2%)
  between operations  1.29 us (1%)
    pallas_call x1, Pallas kernels, shards(): pl.pallas_call(functools.partial(kernel, (nb, nr, groups)), name='primal_...  97.3 us
    unnamed x4, local copies, waits for them, and re-layouts  2.52 us

profile of v1, /device:TPU:0, one launch (start us, length us, event | category | flops | bytes accessed | tf_op | source)
XLA Modules:
  0.0 101.1 jit_solution(16813294480787854311)
XLA Ops:
  1.3 97.3 %primal_dual.1 = (f32[768,128]{1,0:T(8,128)}, f32[512,128]{1,0:T(8,128)}) custom-call(s32[1,1,6]{2,1,0:T(1,128)} %slots_ref.1, s32[1,1]{1,0:T(1,128)S(6)} %copy.10.count_ref, bf16[1,1,6,256,256]{4,3,2,1,0:T(8,128)(2,1)} %tiles_ref.1, f32[768,128]{1,0:T(8,128)} %cost_ref.1, f32[768,128]{1,0:T(8,128)} %x0_ref.1, f32[512,128]{1,0:T(8,128)} %y0_ref.1), custom_call_target="tpu_custom_call" | custom-call | tf_op jit(solution)/shard_map/primal_dual/pallas_call | solution.py:417
  98.6 0.0 copy-start
  98.6 1.8 %copy.11 = f32[768,128]{1,0:T(8,128)} copy(f32[768,128]{1,0:T(8,128)} %get-tuple-element.4) | data formatting | bytes 786432
  100.4 0.0 copy-done
  100.4 0.7 copy.12
Async XLA Ops:
  98.6 1.8 %copy-start = (f32[512,128]{1,0:T(8,128)S(1)}, f32[512,128]{1,0:T(8,128)}, u32[]{:S(2)}) copy-start(f32[512,128]{1,0:T(8,128)} %get-tuple-element.5) | copy-start | bytes 786436

commit v2 on v1

v2 whole, which is shorter than its diff:
```python
import functools

import jax
import jax.numpy as jnp
from jax import lax
from jax.experimental import pallas as pl
from jax.experimental.pallas import tpu as pltpu
from jax.sharding import PartitionSpec as P

ROUNDS = 3
ITERS = 4
eps = 1e-06
GROUPS = 4
SHIFT = 2.2
CROSS = 4.4
CAST = 4.2
FLAT = 64
DOWN = 2.0**-24
UP = 2.0**24
MESH = pl.DeviceIdType.MESH
f32 = jnp.float32
bf16 = jnp.bfloat16


def kernel(
    cfg, slots_ref, count_ref, tiles_ref, cost_ref, x0_ref, y0_ref, primal_ref, dual_ref,
    a_ref, at_ref, tile_s, tile_r, stage, ystage, cost_t, x_t, y_t, part, others, casts, fin, yfin,
    rpeak_s, rpeak_r, cpeak_s, cpeak_r, fr_s, fr_r, fb_s, fb_r, col_s, col_r, row_s, row_r,
    rp_ss, rp_rs, cp_ss, cp_rs, fr_ss, fr_rs, fb_ss, fb_rs,
    g_ss, g_rs, h_ss, h_rs, pair_ss, pair_rs, bulk_ss, bulk_rs, fwd_ss, fwd_rs,
    xf_ss, xf_rs, yf_ss, yf_rs,
):
    nb, nr, groups = cfg
    z = lax.axis_index("band")
    r = lax.axis_index("roster")
    core = r % 2
    chip = r // 2
    chips = nr // 2
    side = z % 2
    slots = tiles_ref.shape[2]
    tile = tiles_ref.shape[3]
    rows, scen = y0_ref.shape
    cols = cost_ref.shape[0]
    col_tiles = cols // tile
    quarter = scen // 4
    per = quarter // groups
    chunks = rows // 128
    flat = nb * nr <= FLAT

    def roster_peer(d):
        return (z, (r + d) % nr)

    def band_peer(d):
        return ((z + d) % nb, r)

    def any_peer(d):
        return ((z + d // nr) % nb, (r + d % nr) % nr)

    def chip_peer(d):
        return (z, 2 * ((chip + d) % chips) + core)

    def pair_peer(d):
        return ((z + 2 * d) % nb, r)

    partner = (z, r + 1 - 2 * core)
    below = (z + 1 - 2 * side, r)
    across = (z + 1 - 2 * side, r + 1 - 2 * core)

    barrier = pltpu.get_barrier_semaphore()
    if flat:
        greet = [any_peer(d) for d in range(1, nb * nr)]
    else:
        greet = [roster_peer(d) for d in range(1, nr)] + [band_peer(d) for d in range(1, nb)] + [across]
    for peer in greet:
        pl.semaphore_signal(barrier, inc=1, device_id=peer, device_id_type=MESH)

    def build():
        for p in range(slots):
            at = jnp.int32(0)
            for s in range(slots):
                at = jnp.where(slots_ref[0, 0, s] == p, jnp.int32(s), at)
            factor = jnp.where(at < count_ref[0, 0], jnp.float32(DOWN), jnp.float32(0.0))
            block = tiles_ref[0, 0, at].astype(f32) * factor
            i, j = (p // col_tiles) * tile, (p % col_tiles) * tile
            tile_s[i : i + tile, j : j + tile] = block
            a_ref[i : i + tile, j : j + tile] = block.astype(bf16)
            at_ref[j : j + tile, i : i + tile] = block.T.astype(bf16)

    def fold(ref, at, span, factor, op):
        part = ref[at : at + 128, :span].astype(f32) * factor
        if op is jnp.add:
            part = part * part
        total = part[:, :128]
        for j in range(128, part.shape[1], 128):
            total = op(total, part[:, j : j + 128])
        return total.T

    def peaks(turn, row, col_up):
        for i in range(0, rows, 128):
            peak = jnp.max(fold(a_ref, i, cols, col_up, jnp.maximum), axis=0, keepdims=True)
            rpeak_s[turn, :, i : i + 128] = peak * row[:, i : i + 128]
        for j in range(0, cols, 128):
            peak = jnp.max(fold(at_ref, j, rows, row, jnp.maximum), axis=0, keepdims=True)
            cpeak_s[turn, :, j : j + 128] = peak * col_up[:, j : j + 128]

    def rpeak_copy(turn, d):
        return pltpu.make_async_remote_copy(
            rpeak_s.at[turn], rpeak_r.at[turn, d], rp_ss.at[turn, d], rp_rs.at[turn, d],
            device_id=roster_peer(d), device_id_type=MESH)

    def cpeak_copy(turn, d):
        return pltpu.make_async_remote_copy(
            cpeak_s.at[turn], cpeak_r.at[turn, d], cp_ss.at[turn, d], cp_rs.at[turn, d],
            device_id=band_peer(d), device_id_type=MESH)

    def peaks_send(turn):
        for d in range(1, nb):
            cpeak_copy(turn, d).start()
        for d in range(1, nr):
            rpeak_copy(turn, d).start()

    def peaks_wait(turn):
        row = rpeak_s[turn]
        col = cpeak_s[turn]
        for d in range(1, nr):
            rpeak_copy(turn, d).wait_recv()
            row = jnp.maximum(row, rpeak_r[turn, d])
        for d in range(1, nb):
            cpeak_copy(turn, d).wait_recv()
            col = jnp.maximum(col, cpeak_r[turn, d])
        return row, col

    firsts = range(1, nb * nr if flat else nr)

    def fr_copy(d):
        return pltpu.make_async_remote_copy(
            fr_s, fr_r.at[d], fr_ss.at[d], fr_rs.at[d],
            device_id=any_peer(d) if flat else roster_peer(d), device_id_type=MESH)

    def fb_copy(d):
        return pltpu.make_async_remote_copy(
            fb_s, fb_r.at[d], fb_ss.at[d], fb_rs.at[d],
            device_id=band_peer(d), device_id_type=MESH)

    def set_at(side, core):
        return pl.ds(pl.multiple_of((2 * side + core) * quarter, 8), quarter)

    def send(i, peer, src, dst):
        return pltpu.make_async_remote_copy(
            src, dst, pair_ss.at[i], pair_rs.at[i], device_id=peer, device_id_type=MESH)

    def tile_copy():
        return send(0, partner, tile_s, tile_r.at[0])

    def cost_copy():
        return send(1, partner, stage.at[0, set_at(side, 1 - core)], cost_t.at[:, cols:])

    def x0_copy():
        return send(2, partner, stage.at[1, set_at(side, 1 - core)], x_t.at[:, cols:])

    def y0_copy():
        return send(3, below, ystage.at[set_at(1 - side, core)], y_t.at[:, rows:])

    def col_copy():
        return send(4, partner, col_s, col_r)

    def row_copy():
        return send(5, below, row_s, row_r)

    def bulk_copy(k):
        at = pl.ds(k * 128, 128)
        return pltpu.make_async_remote_copy(
            tile_s.at[at], tile_r.at[1, at], bulk_ss.at[k], bulk_rs.at[k],
            device_id=below, device_id_type=MESH)

    def fwd_copy(k):
        at = pl.ds(k * 128, 128)
        return pltpu.make_async_remote_copy(
            tile_r.at[1, at], tile_r.at[2, at], fwd_ss.at[k], fwd_rs.at[k],
            device_id=partner, device_id_type=MESH)

    def of(grp):
        return pl.ds(grp * per, per)

    def g_copy(grp, t, d):
        return pltpu.make_async_remote_copy(
            part.at[of(grp)], others.at[t % 2, d, of(grp)],
            g_ss.at[grp, d], g_rs.at[t % 2, grp, d],
            device_id=pair_peer(d), device_id_type=MESH)

    def h_copy(grp, t, d):
        here = casts.at[t % 2, chip, of(grp)]
        return pltpu.make_async_remote_copy(
            here, here, h_ss.at[grp, d], h_rs.at[t % 2, grp, d],
            device_id=chip_peer(d), device_id_type=MESH)

    def h_arrived(grp, t, d):
        here = casts.at[t % 2, (chip + chips - d) % chips, of(grp)]
        return pltpu.make_async_remote_copy(
            here, here, h_ss.at[grp, d], h_rs.at[t % 2, grp, d],
            device_id=chip_peer(d), device_id_type=MESH)

    def final_at(grp):
        return pl.ds(pl.multiple_of((2 * side + core) * quarter + grp * per, 8), per)

    def x_copy(grp, i):
        src = x_t.at[of(grp), :cols] if i == 1 else x_t.at[of(grp), cols:]
        return pltpu.make_async_remote_copy(
            src, fin.at[final_at(grp)], xf_ss.at[grp, i], xf_rs.at[grp, i],
            device_id=(partner, below, across)[i], device_id_type=MESH)

    def y_copy(grp, i):
        src = y_t.at[of(grp), :rows] if i == 0 else y_t.at[of(grp), rows:]
        return pltpu.make_async_remote_copy(
            src, yfin.at[final_at(grp)], yf_ss.at[grp, i], yf_rs.at[grp, i],
            device_id=(partner, below, across)[i], device_id_type=MESH)

    def split_dot(value, matrix):
        high = value.astype(bf16)
        low = (value - high.astype(f32)).astype(bf16)
        both = jnp.dot(jnp.concatenate([high, low], 0), matrix, preferred_element_type=f32)
        return both[: value.shape[0]] + both[value.shape[0] :]

    state = {}

    def begin():
        state["row"] = jnp.ones((1, rows), f32)
        state["col_up"] = jnp.ones((1, cols), f32) * UP
        build()
        peaks(0, state["row"], state["col_up"])
        pl.semaphore_wait(barrier, len(greet))
        peaks_send(0)
        tile_copy().start()
        bulk_copy(0).start()

    def starts():
        for i in range(0, rows, 128):
            ystage[:, i : i + 128] = y0_ref[i : i + 128, :].T
        y0_copy().start()
        y_t[:, :rows] = ystage[set_at(side, core)]
        for i, ref in enumerate((cost_ref, x0_ref)):
            for j in range(0, cols, 128):
                stage[i, :, j : j + 128] = ref[j : j + 128, :].T
        cost_copy().start()
        x0_copy().start()
        cost_t[:, :cols] = stage[0, set_at(side, core)]
        x_t[:, :cols] = stage[1, set_at(side, core)]

    def place(block, i, j, high):
        a_ref[i : i + high, j : j + tile] = block.astype(bf16)
        at_ref[j : j + tile, i : i + high] = block.T.astype(bf16)

    def tiles_in():
        tile_copy().wait_recv()
        for i in range(0, rows, 128):
            for j in range(0, cols, tile):
                place(tile_r[0, i : i + 128, j : j + tile], i, cols + j, 128)

    def bulk_in(k):
        bulk_copy(k).wait_recv()
        fwd_copy(k).start()
        for j in range(0, cols, tile):
            place(tile_r[1, k * 128 : (k + 1) * 128, j : j + tile], rows + k * 128, j, 128)

    def fwd_in(k):
        fwd_copy(k).wait_recv()
        for j in range(0, cols, tile):
            place(tile_r[2, k * 128 : (k + 1) * 128, j : j + tile], rows + k * 128, cols + j, 128)

    def equilibrate(turn):
        row_peak, col_peak = peaks_wait(turn)
        state["row"] = state["row"] / jnp.sqrt(row_peak + eps)
        state["col_up"] = state["col_up"] / jnp.sqrt(col_peak + eps)
        if turn + 1 < ROUNDS:
            peaks(turn + 1, state["row"], state["col_up"])
            peaks_send(turn + 1)
        else:
            squares_start()

    def squares_start():
        row, col_up = state["row"], state["col_up"]
        squares = jnp.zeros((1, 128), f32)
        for j in range(0, cols, 128):
            part = jnp.sum(fold(at_ref, j, rows, row, jnp.add), axis=0, keepdims=True)
            scale = col_up[:, j : j + 128]
            squares = squares + part * scale * scale
        fr_s[...] = squares
        for d in reversed(firsts):
            fr_copy(d).start()
        state["squares"] = squares
        row_s[...] = row
        row_copy().start()
        col_s[...] = col_up
        col_copy().start()

    def squares_end():
        squares = state["squares"]
        for d in firsts:
            fr_copy(d).wait_recv()
            squares = squares + fr_r[d]
        if not flat:
            fb_s[...] = squares
            for d in range(1, nb):
                fb_copy(d).start()
            for d in range(1, nb):
                fb_copy(d).wait_recv()
                squares = squares + fb_r[d]
        eta = 0.9 / jnp.sqrt(jnp.sum(squares, axis=1, keepdims=True) + eps)
        col_copy().wait_recv()
        row_copy().wait_recv()
        up = jnp.concatenate([state["col_up"], col_r[...]], 1)
        wide = jnp.concatenate([state["row"], row_r[...]], 1)
        col = up * DOWN
        state["up"], state["wide"], state["wide_up"] = up, wide, wide * UP
        state["eta_col"], state["eta_row"] = eta * col, eta * wide
        cost_copy().wait_recv()
        x0_copy().wait_recv()
        cost_t[...] = cost_t[...] * col

    def scatter(grp, t):
        if t > 0:
            for d in range(1, nb // 2):
                g_copy(grp, t - 1, d).wait_send()
        part[of(grp), :] = split_dot(y_t[of(grp), :], a_ref[...])
        for d in range(1, nb // 2):
            g_copy(grp, t, d).start()

    def cast(grp, t):
        total = part[of(grp), :]
        for d in range(1, nb // 2):
            g_copy(grp, t, d).wait_recv()
            total = total + others[t % 2, d, of(grp)]
        before = x_t[of(grp), :]
        move = state["eta_col"] * (cost_t[of(grp), :] - state["up"] * total)
        after = jnp.clip(before - move, 0.0, 1.0)
        x_t[of(grp), :] = after
        if t > 0:
            for d in range(1, chips):
                h_copy(grp, t - 1, d).wait_send()
        casts[t % 2, chip, of(grp)] = split_dot(2.0 * after - before, at_ref[...])
        for d in range(1, chips):
            h_copy(grp, t, d).start()
        if t + 1 == ITERS:
            for i in range(3):
                x_copy(grp, i).start()

    def rise(grp, t):
        for d in range(1, chips):
            h_arrived(grp, t, d).wait_recv()
        total = casts[t % 2, 0, of(grp)]
        for k in range(1, chips):
            total = total + casts[t % 2, k, of(grp)]
        wide, wide_up, eta_row = state["wide"], state["wide_up"], state["eta_row"]
        y_t[of(grp), :] = y_t[of(grp), :] + eta_row * (wide - wide_up * total)
        if t + 1 < ITERS:
            scatter(grp, t + 1)
        else:
            for i in range(3):
                y_copy(grp, i).start()

    def bulk_start(k):
        bulk_copy(k).start()

    begin()
    starts()
    tiles_in()
    equilibrate(0)
    bulk_start(1)
    bulk_in(0)
    equilibrate(1)
    bulk_start(2)
    fwd_in(0)
    bulk_in(1)
    equilibrate(2)
    for k in range(3, chunks):
        bulk_copy(k).start()
    fwd_in(1)
    bulk_in(2)
    squares_end()
    fwd_in(2)
    for k in range(3, chunks):
        bulk_in(k)
    y0_copy().wait_recv()
    for k in range(3, chunks):
        fwd_in(k)

    plan = []

    def put(when, step, *args):
        plan.append((when, len(plan), functools.partial(step, *args)))

    for grp in range(groups):
        when = grp * SHIFT
        put(-1.0, scatter, grp, 0)
        for t in range(ITERS):
            put(when, cast, grp, t)
            when += CAST
            put(when, rise, grp, t)
            when += CROSS
    for when, index, step in sorted(plan, key=lambda entry: entry[:2]):
        step()

    col = state["col_up"] * DOWN
    row = state["row"]

    def finish_x():
        fin[set_at(side, core), :] = x_t[:, :cols]
        for grp in range(groups):
            for i in range(3):
                x_copy(grp, i).wait_recv()
        for j in range(0, cols, 128):
            primal_ref[j : j + 128, :] = (fin[:, j : j + 128] / col[:, j : j + 128]).T

    def finish_y():
        yfin[set_at(side, core), :] = y_t[:, :rows]
        for grp in range(groups):
            for i in range(3):
                y_copy(grp, i).wait_recv()
        for i in range(0, rows, 128):
            dual_ref[i : i + 128, :] = (yfin[:, i : i + 128] / row[:, i : i + 128]).T

    finish_x()
    finish_y()

    for copy in (tile_copy, cost_copy, x0_copy, y0_copy, col_copy, row_copy):
        copy().wait_send()
    for k in range(chunks):
        bulk_copy(k).wait_send()
        fwd_copy(k).wait_send()
    for grp in range(groups):
        for i in range(3):
            x_copy(grp, i).wait_send()
            y_copy(grp, i).wait_send()
        for d in range(1, nb // 2):
            g_copy(grp, ITERS - 1, d).wait_send()
        for d in range(1, chips):
            h_copy(grp, ITERS - 1, d).wait_send()
    for d in firsts:
        fr_copy(d).wait_send()
    for turn in range(ROUNDS):
        for d in range(1, nr):
            rpeak_copy(turn, d).wait_send()
        for d in range(1, nb):
            cpeak_copy(turn, d).wait_send()
    if not flat:
        for d in range(1, nb):
            fb_copy(d).wait_send()


def shards(nb, nr, tiles, tile_slots, tile_count, costs, primal_start, dual_start):
    rows, scen = dual_start.shape
    cols = costs.shape[0]
    groups = GROUPS
    quarter = scen // 4
    chips = nr // 2
    chunks = rows // 128
    firsts = nb * nr if nb * nr <= FLAT else nr
    vmem = pl.BlockSpec(memory_space=pltpu.VMEM)
    smem = pl.BlockSpec(memory_space=pltpu.SMEM)
    dma = pltpu.SemaphoreType.DMA
    return pl.pallas_call(
        functools.partial(kernel, (nb, nr, groups)),
        name="primal_dual",
        out_shape=(
            jax.ShapeDtypeStruct((cols, scen), f32),
            jax.ShapeDtypeStruct((rows, scen), f32),
        ),
        in_specs=[smem, smem, vmem, vmem, vmem, vmem],
        out_specs=(vmem, vmem),
        scratch_shapes=[
            pltpu.VMEM((2 * rows, 2 * cols), bf16),
            pltpu.VMEM((2 * cols, 2 * rows), bf16),
            pltpu.VMEM((rows, cols), f32),
            pltpu.VMEM((3, rows, cols), f32),
            pltpu.VMEM((2, scen, cols), f32),
            pltpu.VMEM((scen, rows), f32),
            pltpu.VMEM((quarter, 2 * cols), f32),
            pltpu.VMEM((quarter, 2 * cols), f32),
            pltpu.VMEM((quarter, 2 * rows), f32),
            pltpu.VMEM((quarter, 2 * cols), f32),
            pltpu.VMEM((2, nb // 2, quarter, 2 * cols), f32),
            pltpu.VMEM((2, chips, quarter, 2 * rows), f32),
            pltpu.VMEM((scen, cols), f32),
            pltpu.VMEM((scen, rows), f32),
            pltpu.VMEM((ROUNDS, 1, rows), f32),
            pltpu.VMEM((ROUNDS, nr, 1, rows), f32),
            pltpu.VMEM((ROUNDS, 1, cols), f32),
            pltpu.VMEM((ROUNDS, nb, 1, cols), f32),
            pltpu.VMEM((1, 128), f32),
            pltpu.VMEM((firsts, 1, 128), f32),
            pltpu.VMEM((1, 128), f32),
            pltpu.VMEM((nb, 1, 128), f32),
            pltpu.VMEM((1, cols), f32),
            pltpu.VMEM((1, cols), f32),
            pltpu.VMEM((1, rows), f32),
            pltpu.VMEM((1, rows), f32),
            dma((ROUNDS, nr)),
            dma((ROUNDS, nr)),
            dma((ROUNDS, nb)),
            dma((ROUNDS, nb)),
            dma((firsts,)),
            dma((firsts,)),
            dma((nb,)),
            dma((nb,)),
            dma((groups, nb // 2)),
            dma((2, groups, nb // 2)),
            dma((groups, chips)),
            dma((2, groups, chips)),
            dma((6,)),
            dma((6,)),
            dma((chunks,)),
            dma((chunks,)),
            dma((chunks,)),
            dma((chunks,)),
            dma((groups, 3)),
            dma((groups, 3)),
            dma((groups, 3)),
            dma((groups, 3)),
        ],
        compiler_params=pltpu.CompilerParams(collective_id=0, has_side_effects=True),
    )(tile_slots, tile_count, tiles, costs, primal_start, dual_start)


def solution(mesh):
    placed = (
        P("band", "roster", None, None, None),
        P("band", "roster", None),
        P("band", "roster"),
        P("roster", None),
        P("roster", None),
        P("band", None),
    )
    return jax.shard_map(
        functools.partial(shards, mesh.shape["band"], mesh.shape["roster"]),
        mesh=mesh,
        in_specs=placed,
        out_specs=(P("roster", None), P("band", None)),
        check_vma=False,
    )
```

time: 101 us -> 107 us (1.059)
  Pallas kernels: 97.3 us -> 103 us
    pallas_call x1, Pallas kernels: 97.3 us -> 103 us  [shards(): pl.pallas_call(functools.partial(kernel, (nb, nr, groups)), name='primal_...]
where the time goes in v2:
time: 107 us
  Pallas kernels  103 us (96%)
  local copies, waits for them, and re-layouts  2.52 us (2%)
  between operations  1.29 us (1%)
    pallas_call x1, Pallas kernels, shards(): pl.pallas_call(functools.partial(kernel, (nb, nr, groups)), name='primal_...  103 us
    unnamed x4, local copies, waits for them, and re-layouts  2.52 us

profile of v2, /device:TPU:0, one launch (start us, length us, event | category | flops | bytes accessed | tf_op | source)
XLA Modules:
  0.0 107.0 jit_solution(13037217960475529223)
XLA Ops:
  1.3 103.2 %primal_dual.1 = (f32[768,128]{1,0:T(8,128)}, f32[512,128]{1,0:T(8,128)}) custom-call(s32[1,1,6]{2,1,0:T(1,128)} %slots_ref.1, s32[1,1]{1,0:T(1,128)S(6)} %copy.10.count_ref, bf16[1,1,6,256,256]{4,3,2,1,0:T(8,128)(2,1)} %tiles_ref.1, f32[768,128]{1,0:T(8,128)} %cost_ref.1, f32[768,128]{1,0:T(8,128)} %x0_ref.1, f32[512,128]{1,0:T(8,128)} %y0_ref.1), custom_call_target="tpu_custom_call" | custom-call | tf_op jit(solution)/shard_map/primal_dual/pallas_call | solution.py:461
  104.5 0.0 copy-start
  104.5 1.8 %copy.11 = f32[768,128]{1,0:T(8,128)} copy(f32[768,128]{1,0:T(8,128)} %get-tuple-element.4) | data formatting | bytes 786432
  106.3 0.0 copy-done
  106.3 0.7 copy.12
Async XLA Ops:
  104.5 1.8 %copy-start = (f32[512,128]{1,0:T(8,128)S(1)}, f32[512,128]{1,0:T(8,128)}, u32[]{:S(2)}) copy-start(f32[512,128]{1,0:T(8,128)} %get-tuple-element.5) | copy-start | bytes 786436
